TPU v7x, 128 devices: a whole 4x4x4 slice. The times are simulated.
128 devices in a mesh: seg: 32 (over z, y, x_lo), band: 4 (over x_hi, core).
Axes of the slice: x: 4 (x_hi: 2, x_lo: 2; x = x_hi * 2 + x_lo), y: 4, z: 4, core: 2. Of those that a mesh axis runs over, the one named last changes fastest.
Arguments:
- latents: bfloat16 [1024, 2560], P(('seg', 'band')), may hold values from -40 to 40
- weight_in: bfloat16 [3, 144, 384], replicated, may hold values from -0.3125 to 0.3125
- weight_mid: bfloat16 [3, 3456, 384], replicated, may hold values from -0.0625 to 0.0625
- weight_up: bfloat16 [3456, 192], replicated, may hold values from -0.109375 to 0.109375
- norm_gain: float32 [384], replicated, may hold values from 0.5 to 1.5
- norm_shift: float32 [384], replicated, may hold values from -2.5 to 2.5
Outputs:
- decoded: bfloat16 [64, 32, 61440], P('seg', 'band')
All inputs are finite; a program needn't handle non-finite values.
Results may differ from a plain program's by a relative error of at most 0.012.
Values may be sent and summed in bfloat16 or wider, within the bound.
A program may use at most 128 MiB of HBM per device.

v0:
```python
import functools

import jax
import jax.numpy as jnp
from jax import lax
from jax.experimental import pallas as pl
from jax.experimental.pallas import tpu as pltpu
from jax.sharding import PartitionSpec as P

C_LAT = 16
C_MID = 384
C_OUT = 192
GROUPS = 32
COLS = 160
HL = 16
FR = 2
RB = 4
BANDS = 4
CELLS = HL * COLS * (C_MID // GROUPS)
TAPW = 3 * C_MID
PAIRS = ((1, 2), (3, 4), (0, 5))
MESH = pl.DeviceIdType.MESH
BF = jnp.bfloat16
F32 = jnp.float32


def col_shifts(v):
    cols = v.shape[0]
    j = lax.broadcasted_iota(jnp.int32, v.shape, 0)
    before = jnp.where(j == 0, 0.0, pltpu.roll(v, 1, 0))
    after = jnp.where(j == cols - 1, 0.0, pltpu.roll(v, cols - 1, 0))
    return before, v, after


def features_kernel(
    segs, z, w_in, w_mid, w_upt, gain, shift, x1_out, u_out,
    lrecv, lst, wb, x0s, wm, gs, st_src, st_recv, v3, x1s,
    wsem, lsend_sem, lrecv_sem, ssend_sem, srecv_sem, hsend_sem, hrecv_sem,
):
    s = lax.axis_index("seg")
    b = lax.axis_index("band")
    half = lax.rem(b, 2)

    load_w = pltpu.make_async_copy(w_mid, wm, wsem)
    load_w.start()

    barrier = pltpu.get_barrier_semaphore()

    def each_peer(fn):
        for ds in range(-2, 3):
            for tb in range(BANDS):
                ok = jnp.logical_and(s + ds >= 0, s + ds < segs)
                if ds == 0:
                    ok = jnp.logical_and(ok, b != tb)
                pl.when(ok)(functools.partial(fn, ds, tb))

    def greet(ds, tb):
        pl.semaphore_signal(barrier, inc=1, device_id={"seg": s + ds, "band": jnp.int32(tb)}, device_id_type=MESH)

    peers = -1
    for ds in range(-2, 3):
        ok = jnp.logical_and(s + ds >= 0, s + ds < segs)
        peers = peers + jnp.where(ok, BANDS, 0)

    each_peer(greet)

    for q, pair in enumerate(PAIRS):
        for k, r in enumerate(pair):
            for t in range(3):
                for dx in range(3):
                    for rw in range(8):
                        dy = rw - r
                        at = t * 384 + dx * 128 + rw * 16
                        if 0 <= dy < 3:
                            blk = w_in[t, (dy * 3 + dx) * 16 : (dy * 3 + dx + 1) * 16, :]
                        else:
                            blk = jnp.zeros((16, C_MID), BF)
                        wb[q, at : at + 16, k * C_MID : (k + 1) * C_MID] = blk

    pl.semaphore_wait(barrier, peers)

    def latent_copy(ds, tb):
        return pltpu.make_async_remote_copy(
            src_ref=z,
            dst_ref=lrecv.at[8 - 4 * ds + b],
            send_sem=lsend_sem.at[ds * BANDS + tb],
            recv_sem=lrecv_sem.at[8 - 4 * ds + b],
            device_id={"seg": s + ds, "band": jnp.int32(tb)},
            device_id_type=MESH,
        )

    def each_latent_copy(fn):
        for ds in range(3):
            for tb in range(BANDS):
                ok = s + ds < segs
                if tb == 0:
                    ok = jnp.logical_and(ok, half == 0)
                if tb == BANDS - 1:
                    ok = jnp.logical_and(ok, half == 1)
                if ds == 0:
                    ok = jnp.logical_and(ok, b != tb)
                pl.when(ok)(functools.partial(fn, ds, tb))

    each_latent_copy(lambda ds, tb: latent_copy(ds, tb).start())
    lrecv[8 + b] = z[...]

    sets = (((0,), (1, 2)), ((0, 1), (2,)))
    for r2 in range(2):
        for c2 in range(2):
            ph = r2 * 2 + c2
            for rt in range(2):
                for ct in range(2):
                    acc = None
                    for dy in sets[r2][rt]:
                        for dx in sets[c2][ct]:
                            w = w_upt[:, (dy * 3 + dx) * C_MID : (dy * 3 + dx + 1) * C_MID].astype(F32)
                            acc = w if acc is None else acc + w
                    k0 = (rt * 2 + ct) * C_MID
                    n0 = 64 * c2
                    u_out[ph, n0 : n0 + C_OUT, k0 : k0 + C_MID] = acc.astype(BF)
            z0 = C_OUT if c2 == 0 else 0
            u_out[ph, z0 : z0 + 64, :] = jnp.zeros((64, 4 * C_MID), BF)

    load_w.wait()

    def combine(i, c):
        rows = pl.ds(pl.multiple_of(i * 128, 128), 128)
        w0, w1, w2 = (wm[t, rows, :].astype(F32) for t in range(3))
        outer, mid = (w0 + w2) * 0.5, w1 * 0.5
        gs[0, rows, :] = (outer + mid).astype(BF)
        gs[1, rows, :] = (outer - mid).astype(BF)
        return c

    lax.fori_loop(0, 27, combine, 0)

    def arrived(slot):
        pltpu.make_async_remote_copy(
            src_ref=z,
            dst_ref=lrecv.at[slot],
            send_sem=lsend_sem.at[0],
            recv_sem=lrecv_sem.at[slot],
            device_id={"seg": s, "band": b},
            device_id_type=MESH,
        ).wait_recv()

    for slot in range(12):
        ok = s - 2 + slot // 4 >= 0
        if slot % 2 == 0:
            ok = jnp.logical_and(ok, b <= 2)
        else:
            ok = jnp.logical_and(ok, b >= 1)
        if slot >= 8:
            ok = jnp.logical_and(ok, b != slot - 8)
        pl.when(ok)(functools.partial(arrived, slot))

    lane = lax.broadcasted_iota(jnp.int32, (COLS, 128), 1)
    row = 4 * b - 2 + lane // 16
    in_frame = jnp.logical_and(row >= 0, row < HL)
    for g in range(6):
        both = jnp.concatenate([lrecv[2 * g].astype(F32), lrecv[2 * g + 1].astype(F32)], axis=1)
        win = pltpu.roll(both, lax.rem(32 - 64 * b + 256, 256), 1)[:, :128]
        win = jnp.where(jnp.logical_and(in_frame, 2 * s - 4 + g >= 0), win, 0.0)
        taps = jnp.concatenate(col_shifts(win), axis=1).astype(BF)
        for f in range(4):
            t = g - f
            if 0 <= t < 3:
                lst[f * COLS : (f + 1) * COLS, t * 384 : (t + 1) * 384] = taps

    def conv_in(q):
        return jnp.dot(lst[...], wb[q], preferred_element_type=F32).astype(BF)

    sums = [[None] * 4, [None] * 4]
    for q, pair in enumerate(PAIRS[:2]):
        x0 = conv_in(q)
        for f in range(4):
            for k, r in enumerate(pair):
                part = x0[f * COLS : (f + 1) * COLS, k * C_MID : (k + 1) * C_MID]
                x0s[f, r] = part
                wide = part.astype(F32)
                for m, v in enumerate((wide, wide * wide)):
                    tot = jnp.sum(v, axis=0, keepdims=True)
                    sums[m][f] = tot if sums[m][f] is None else sums[m][f] + tot
    st_src[...] = jnp.concatenate(sums[0] + sums[1], axis=0)

    def stat_copy(tb):
        return pltpu.make_async_remote_copy(
            src_ref=st_src,
            dst_ref=st_recv.at[b],
            send_sem=ssend_sem.at[tb],
            recv_sem=srecv_sem.at[b],
            device_id={"seg": s, "band": jnp.int32(tb)},
            device_id_type=MESH,
        )

    for tb in range(BANDS):
        pl.when(b != tb)(lambda tb=tb: stat_copy(tb).start())
    st_recv[b] = st_src[...]

    x0 = conv_in(2)
    for f in range(4):
        for k, r in enumerate(PAIRS[2]):
            x0s[f, r] = x0[f * COLS : (f + 1) * COLS, k * C_MID : (k + 1) * C_MID]

    def stats_in(ob):
        pltpu.make_async_remote_copy(
            src_ref=st_src,
            dst_ref=st_recv.at[ob],
            send_sem=ssend_sem.at[0],
            recv_sem=srecv_sem.at[ob],
            device_id={"seg": s, "band": b},
            device_id_type=MESH,
        ).wait_recv()

    for ob in range(BANDS):
        pl.when(b != ob)(functools.partial(stats_in, ob))

    total = (st_recv[0] + st_recv[1]) + (st_recv[2] + st_recv[3])
    per = C_MID // GROUPS
    gi = lax.broadcasted_iota(jnp.int32, (C_MID, C_MID), 0) // per
    gj = lax.broadcasted_iota(jnp.int32, (C_MID, C_MID), 1) // per
    same = jnp.where(gi == gj, 1.0, 0.0).astype(F32)
    total = jnp.dot(total, same, preferred_element_type=F32, precision=lax.Precision.HIGHEST)
    mean = total[0:4] / CELLS
    rstd = lax.rsqrt(total[4:8] / CELLS - mean * mean + 1e-6)
    mul = rstd * gain[...].reshape(1, C_MID)
    add = shift[...].reshape(1, C_MID) - mean * mul

    def activate(r, c):
        arow = 4 * b - 1 + r
        row_ok = jnp.logical_and(arow >= 0, arow < HL)
        a = []
        for f in range(4):
            ok = jnp.logical_and(row_ok, 2 * s - 2 + f >= 0)
            v = x0s[f, r].astype(F32) * mul[f : f + 1] + add[f : f + 1]
            hv = 0.5 * v
            act = hv + hv * jnp.tanh(hv)
            a.append(jnp.where(ok, act, 0.0))
        for i, v in enumerate((a[0] - a[2], a[1] + a[2], a[2] - a[1], a[1] - a[3])):
            for dx, w in enumerate(col_shifts(v)):
                v3[i, r, :, dx * C_MID : (dx + 1) * C_MID] = w.astype(BF)
        return c

    lax.fori_loop(0, 6, activate, 0)

    def halo_copy(up):
        return pltpu.make_async_remote_copy(
            src_ref=x1s.at[:, 1 if up else RB],
            dst_ref=x1s.at[:, RB + 1 if up else 0],
            send_sem=hsend_sem.at[0 if up else 1],
            recv_sem=hrecv_sem.at[0 if up else 1],
            device_id={"seg": s, "band": b - 1 if up else b + 1},
            device_id_type=MESH,
        )

    def residual(h, c):
        ra, rb = h, 3 - h

        def product(i):
            acc = None
            for dy in range(3):
                x = jnp.concatenate([v3[i, ra + dy], v3[i, rb + dy]], axis=0)
                ks = slice(dy * TAPW, (dy + 1) * TAPW)
                g = (wm[0, ks, :], gs[0, ks, :], gs[1, ks, :], wm[2, ks, :])[i]
                d = jnp.dot(x, g, preferred_element_type=F32)
                acc = d if acc is None else acc + d
            return acc

        t1, t2, t3, t4 = (product(i) for i in range(4))
        for f, y in enumerate((t1 + t2 + t3, t2 - t3 - t4)):
            x1s[f, 1 + ra] = (x0s[FR + f, 1 + ra].astype(F32) + y[:COLS]).astype(BF)
            x1s[f, 1 + rb] = (x0s[FR + f, 1 + rb].astype(F32) + y[COLS:]).astype(BF)

        @pl.when(h == 0)
        def _():
            pl.when(b > 0)(lambda: halo_copy(True).start())
            pl.when(b < BANDS - 1)(lambda: halo_copy(False).start())

        return c

    lax.fori_loop(0, 2, residual, 0)

    @pl.when(b > 0)
    def _():
        halo_copy(False).wait_recv()

    @pl.when(b < BANDS - 1)
    def _():
        halo_copy(True).wait_recv()

    x1_out[:, 1 : RB + 1] = x1s[:, 1 : RB + 1]
    nothing = jnp.zeros((FR, COLS, C_MID), BF)
    x1_out[:, 0] = jnp.where(b > 0, x1s[:, 0], nothing)
    x1_out[:, RB + 1] = jnp.where(b < BANDS - 1, x1s[:, RB + 1], nothing)

    pl.when(b > 0)(lambda: halo_copy(True).wait_send())
    pl.when(b < BANDS - 1)(lambda: halo_copy(False).wait_send())
    each_latent_copy(lambda ds, tb: latent_copy(ds, tb).wait_send())
    for tb in range(BANDS):
        pl.when(b != tb)(lambda tb=tb: stat_copy(tb).wait_send())


def upsample_kernel(x1, u, out, x3, zs):
    def widen(r, c):
        v = x1[0, r].astype(F32)
        for dx, w in enumerate(col_shifts(v)):
            x3[r, :, dx * C_MID : (dx + 1) * C_MID] = w.astype(BF)
        return c

    lax.fori_loop(0, RB + 2, widen, 0)
    for r2 in range(2):
        y = []
        for c2 in range(2):
            acc = None
            for rt in range(2):
                x = x3[r2 + rt : r2 + rt + RB, :, c2 * C_MID : (c2 + 2) * C_MID].reshape(RB * COLS, 2 * C_MID)
                d = lax.dot_general(
                    x, u[r2 * 2 + c2, :, rt * 2 * C_MID : (rt + 1) * 2 * C_MID],
                    (((1,), (1,)), ((), ())), preferred_element_type=F32,
                )
                acc = d if acc is None else acc + d
            y.append(acc)
        full = jnp.concatenate([y[0][:, :128], y[0][:, 128:] + y[1][:, :128], y[1][:, 128:]], axis=1)
        for p in range(RB):
            for l in range(3):
                zs[l, pl.ds(2 * p + r2, COLS, stride=8), :] = full[p * COLS : (p + 1) * COLS, l * 128 : (l + 1) * 128]

    for q in range(COLS):
        for l in range(3):
            at = q * 2 * C_OUT + l * 128
            out[0, :, at : at + 128] = zs[l, q * 8 : (q + 1) * 8, :].astype(BF)


def local(segs, latents, weight_in, weight_mid, weight_up, norm_gain, norm_shift):
    z = latents.reshape(8, COLS, C_LAT).transpose(1, 0, 2).reshape(COLS, 8 * C_LAT)
    vm = pl.BlockSpec(memory_space=pltpu.VMEM)
    x1, u = pl.pallas_call(
        functools.partial(features_kernel, segs),
        out_shape=(
            jax.ShapeDtypeStruct((FR, RB + 2, COLS, C_MID), BF),
            jax.ShapeDtypeStruct((4, 256, 4 * C_MID), BF),
        ),
        in_specs=[vm, vm, pl.BlockSpec(memory_space=pl.ANY), vm, vm, vm],
        out_specs=(vm, vm),
        scratch_shapes=[
            pltpu.VMEM((12, COLS, 128), BF),
            pltpu.VMEM((4 * COLS, 3 * 384), BF),
            pltpu.VMEM((3, 3 * 384, 2 * C_MID), BF),
            pltpu.VMEM((4, RB + 2, COLS, C_MID), BF),
            pltpu.VMEM((3, 9 * C_MID, C_MID), BF),
            pltpu.VMEM((2, 9 * C_MID, C_MID), BF),
            pltpu.VMEM((8, C_MID), F32),
            pltpu.VMEM((BANDS, 8, C_MID), F32),
            pltpu.VMEM((4, RB + 2, COLS, TAPW), BF),
            pltpu.VMEM((FR, RB + 2, COLS, C_MID), BF),
            pltpu.SemaphoreType.DMA,
            pltpu.SemaphoreType.DMA((12,)),
            pltpu.SemaphoreType.DMA((12,)),
            pltpu.SemaphoreType.DMA((BANDS,)),
            pltpu.SemaphoreType.DMA((BANDS,)),
            pltpu.SemaphoreType.DMA((2,)),
            pltpu.SemaphoreType.DMA((2,)),
        ],
        compiler_params=pltpu.CompilerParams(collective_id=0, has_side_effects=True, vmem_limit_bytes=56 << 20),
        name="features",
    )(z, weight_in, weight_mid, weight_up.T, norm_gain, norm_shift)
    return pl.pallas_call(
        upsample_kernel,
        grid=(FR,),
        out_shape=jax.ShapeDtypeStruct((FR, 2 * RB, 2 * COLS * C_OUT), BF),
        in_specs=[
            pl.BlockSpec((1, RB + 2, COLS, C_MID), lambda f: (f, 0, 0, 0)),
            pl.BlockSpec((4, 256, 4 * C_MID), lambda f: (0, 0, 0)),
        ],
        out_specs=pl.BlockSpec((1, 2 * RB, 2 * COLS * C_OUT), lambda f: (f, 0, 0)),
        scratch_shapes=[
            pltpu.VMEM((RB + 2, COLS, TAPW), BF),
            pltpu.VMEM((3, COLS * 8, 128), F32),
        ],
        compiler_params=pltpu.CompilerParams(vmem_limit_bytes=40 << 20),
        name="upsample",
    )(x1, u)


def solution(mesh):
    return jax.shard_map(
        functools.partial(local, mesh.shape["seg"]),
        mesh=mesh,
        in_specs=(P(("seg", "band"), None), P(), P(), P(), P(), P()),
        out_specs=P("seg", "band", None),
        check_vma=False,
    )
```

profile of v0, /device:TPU:65, one launch (start us, length us, event | category | flops | bytes accessed | tf_op | source)
XLA Modules:
  0.0 50.3 jit_solution(4102686646645110006)
XLA Ops:
  0.0 1.1 %reshape.6 = bf16[8,160,16]{2,1,0:T(8,128)(2,1)S(1)} reshape(bf16[8,2560]{1,0:T(8,128)(2,1)} %param.6) | data formatting | bytes 81920 | tf_op jit(solution)/shard_map/reshape | solution.py:334
  1.1 0.2 copy.8
  1.2 0.7 %copy.9.z = bf16[160,128]{1,0:T(8,128)(2,1)} copy(bf16[160,128]{0,1:T(8,128)(2,1)S(1)} %bitcast.5) | data formatting | bytes 81920 | tf_op jit(solution)/shard_map/reshape | solution.py:334
  2.0 38.2 %features.1 = (bf16[2,6,160,384]{3,2,1,0:T(8,128)(2,1)}, bf16[4,256,1536]{2,1,0:T(8,128)(2,1)}) custom-call(bf16[160,128]{1,0:T(8,128)(2,1)} %copy.9.z, bf16[3,144,384]{2,1,0:T(8,128)(2,1)} %w_in.1, bf16[3,3456,384]{2,1,0:T(8,128)(2,1)} %w_mid.1, bf16[192,3456]{1,0:T(8,128)(2,1)} %bitcast.3, f32[384]{0:T(512)} %gain.1, f32[384]{0:T(512)} %shift.1), custom_call_target="tpu_custom_call" | custom-call | tf_op jit(solution)/shard_map/features/pallas_call | solution.py:336
  40.2 0.0 copy-start
  40.2 1.9 %copy-done = bf16[4,256,1536]{2,1,0:T(8,128)(2,1)S(1)} copy-done((bf16[4,256,1536]{2,1,0:T(8,128)(2,1)S(1)}, bf16[4,256,1536]{2,1,0:T(8,128)(2,1)}, u32[]{:S(2)}) %copy-start) | copy-done | bytes 3145752
  42.1 0.0 copy-start.1
  42.1 1.4 %copy-done.1 = bf16[2,6,160,384]{3,2,1,0:T(8,128)(2,1)S(1)} copy-done((bf16[2,6,160,384]{3,2,1,0:T(8,128)(2,1)S(1)}, bf16[2,6,160,384]{3,2,1,0:T(8,128)(2,1)}, u32[]{:S(2)}) %copy-start.1) | copy-done | bytes 1474584
  43.5 6.8 %upsample.1 = bf16[2,8,61440]{2,1,0:T(8,128)(2,1)} custom-call(bf16[2,6,160,384]{3,2,1,0:T(8,128)(2,1)S(1)} %copy-done.1, bf16[4,256,1536]{2,1,0:T(8,128)(2,1)S(1)} %copy-done), custom_call_target="tpu_custom_call" | custom-call | tf_op jit(solution)/shard_map/upsample/pallas_call | solution.py:366
Async XLA Ops:
  40.2 1.9 %copy-start = (bf16[4,256,1536]{2,1,0:T(8,128)(2,1)S(1)}, bf16[4,256,1536]{2,1,0:T(8,128)(2,1)}, u32[]{:S(2)}) copy-start(bf16[4,256,1536]{2,1,0:T(8,128)(2,1)} %get-tuple-element.8.u) | copy-start | bytes 9437188
  42.1 1.4 %copy-start.1 = (bf16[2,6,160,384]{3,2,1,0:T(8,128)(2,1)S(1)}, bf16[2,6,160,384]{3,2,1,0:T(8,128)(2,1)}, u32[]{:S(2)}) copy-start(bf16[2,6,160,384]{3,2,1,0:T(8,128)(2,1)} %get-tuple-element.7.x1) | copy-start | bytes 4423684
where the time goes:
time: 50.7 us; the launch traced here: 50.3 us
  Pallas kernels  45.1 us (89%)
  local copies, waits for them, and re-layouts  5.22 us (10%)
    pallas_call x1, Pallas kernels, local(): pl.pallas_call(functools.partial(features_kernel, segs), out_shape=(jax.S...  38.2 us
    pallas_call x1, Pallas kernels, local(): pl.pallas_call(upsample_kernel, grid=(FR,), out_shape=jax.ShapeDtypeStruc...  6.81 us
    unnamed x4, local copies, waits for them, and re-layouts  3.26 us
    reshape x2, local copies, waits for them, and re-layouts, local(): latents.reshape(8, COLS, C_LAT).transpose(1, 0, 2).reshape(COLS, 8 * C_LAT)  1.78 us

commit v1 on v0

--- a/solution.py
+++ b/solution.py
@@ -32,17 +32,36 @@
     return before, v, after
 
 
-def features_kernel(
-    segs, z, w_in, w_mid, w_upt, gain, shift, x1_out, u_out,
-    lrecv, lst, wb, x0s, wm, gs, st_src, st_recv, v3, x1s,
+def columns_first(lat):
+    blocks = COLS * C_LAT // 128
+    x = jnp.concatenate([lat[:, k * 128 : (k + 1) * 128].astype(F32)[None] for k in range(blocks)], axis=0)
+    row = lax.broadcasted_iota(jnp.int32, x.shape, 1)
+    col = lax.broadcasted_iota(jnp.int32, x.shape, 2) // C_LAT
+    for k in (1, 2, 4):
+        r, c = (row // k) % 2, (col // k) % 2
+        from_below = pltpu.roll(pltpu.roll(x, k * C_LAT, 2), 8 - k, 1)
+        from_above = pltpu.roll(pltpu.roll(x, 128 - k * C_LAT, 2), k, 1)
+        x = jnp.where(r == c, x, jnp.where(r < c, from_below, from_above))
+    return x.reshape(COLS, 128).astype(BF)
+
+
+def decoder_kernel(
+    segs, lat_hbm, w_in_hbm, w_mid, w_up_hbm, gain_hbm, shift_hbm, out,
+    lat, gain, shift, w_in, w_upt, z, lrecv, lst, wb, x0s, wm, gs, st_src, st_recv, v3, x1s, u, x3, zs,
     wsem, lsend_sem, lrecv_sem, ssend_sem, srecv_sem, hsend_sem, hrecv_sem,
 ):
     s = lax.axis_index("seg")
     b = lax.axis_index("band")
     half = lax.rem(b, 2)
 
-    load_w = pltpu.make_async_copy(w_mid, wm, wsem)
-    load_w.start()
+    load_in = pltpu.make_async_copy(w_in_hbm, w_in, wsem.at[0])
+    load_up = pltpu.make_async_copy(w_up_hbm, w_upt, wsem.at[1])
+    load_w = pltpu.make_async_copy(w_mid, wm, wsem.at[2])
+    load_lat = pltpu.make_async_copy(lat_hbm, lat, wsem.at[3])
+    load_gain = pltpu.make_async_copy(gain_hbm, gain, wsem.at[4])
+    load_shift = pltpu.make_async_copy(shift_hbm, shift, wsem.at[5])
+    for load in (load_lat, load_in, load_up, load_w, load_gain, load_shift):
+        load.start()
 
     barrier = pltpu.get_barrier_semaphore()
 
@@ -63,7 +82,10 @@
         peers = peers + jnp.where(ok, BANDS, 0)
 
     each_peer(greet)
-
+    load_lat.wait()
+    z[...] = columns_first(lat)
+
+    load_in.wait()
     for q, pair in enumerate(PAIRS):
         for k, r in enumerate(pair):
             for t in range(3):
@@ -104,6 +126,7 @@
     each_latent_copy(lambda ds, tb: latent_copy(ds, tb).start())
     lrecv[8 + b] = z[...]
 
+    load_up.wait()
     sets = (((0,), (1, 2)), ((0, 1), (2,)))
     for r2 in range(2):
         for c2 in range(2):
@@ -117,9 +140,9 @@
                             acc = w if acc is None else acc + w
                     k0 = (rt * 2 + ct) * C_MID
                     n0 = 64 * c2
-                    u_out[ph, n0 : n0 + C_OUT, k0 : k0 + C_MID] = acc.astype(BF)
+                    u[ph, n0 : n0 + C_OUT, k0 : k0 + C_MID] = acc.astype(BF)
             z0 = C_OUT if c2 == 0 else 0
-            u_out[ph, z0 : z0 + 64, :] = jnp.zeros((64, 4 * C_MID), BF)
+            u[ph, z0 : z0 + 64, :] = jnp.zeros((64, 4 * C_MID), BF)
 
     load_w.wait()
 
@@ -222,19 +245,20 @@
     total = jnp.dot(total, same, preferred_element_type=F32, precision=lax.Precision.HIGHEST)
     mean = total[0:4] / CELLS
     rstd = lax.rsqrt(total[4:8] / CELLS - mean * mean + 1e-6)
+    load_gain.wait()
+    load_shift.wait()
     mul = rstd * gain[...].reshape(1, C_MID)
-    add = shift[...].reshape(1, C_MID) - mean * mul
+    add = (shift[...].reshape(1, C_MID) - mean * mul) * 0.5
+    mul = mul * 0.5
 
     def activate(r, c):
         arow = 4 * b - 1 + r
         row_ok = jnp.logical_and(arow >= 0, arow < HL)
         a = []
         for f in range(4):
-            ok = jnp.logical_and(row_ok, 2 * s - 2 + f >= 0)
-            v = x0s[f, r].astype(F32) * mul[f : f + 1] + add[f : f + 1]
-            hv = 0.5 * v
-            act = hv + hv * jnp.tanh(hv)
-            a.append(jnp.where(ok, act, 0.0))
+            ok = jnp.where(jnp.logical_and(row_ok, 2 * s - 2 + f >= 0), 1.0, 0.0)
+            hv = x0s[f, r].astype(F32) * (mul[f : f + 1] * ok) + add[f : f + 1] * ok
+            a.append(hv + hv * jnp.tanh(hv))
         for i, v in enumerate((a[0] - a[2], a[1] + a[2], a[2] - a[1], a[1] - a[3])):
             for dx, w in enumerate(col_shifts(v)):
                 v3[i, r, :, dx * C_MID : (dx + 1) * C_MID] = w.astype(BF)
@@ -252,6 +276,10 @@
             device_id_type=MESH,
         )
 
+    def widen(f, r, v):
+        for dx, w in enumerate(col_shifts(v)):
+            x3[f, r, :, dx * C_MID : (dx + 1) * C_MID] = w.astype(BF)
+
     def residual(h, c):
         ra, rb = h, 3 - h
 
@@ -267,8 +295,10 @@
 
         t1, t2, t3, t4 = (product(i) for i in range(4))
         for f, y in enumerate((t1 + t2 + t3, t2 - t3 - t4)):
-            x1s[f, 1 + ra] = (x0s[FR + f, 1 + ra].astype(F32) + y[:COLS]).astype(BF)
-            x1s[f, 1 + rb] = (x0s[FR + f, 1 + rb].astype(F32) + y[COLS:]).astype(BF)
+            for r, part in ((ra, y[:COLS]), (rb, y[COLS:])):
+                x1 = (x0s[FR + f, 1 + r].astype(F32) + part).astype(BF)
+                x1s[f, 1 + r] = x1
+                widen(f, 1 + r, x1.astype(F32))
 
         @pl.when(h == 0)
         def _():
@@ -287,10 +317,34 @@
     def _():
         halo_copy(True).wait_recv()
 
-    x1_out[:, 1 : RB + 1] = x1s[:, 1 : RB + 1]
-    nothing = jnp.zeros((FR, COLS, C_MID), BF)
-    x1_out[:, 0] = jnp.where(b > 0, x1s[:, 0], nothing)
-    x1_out[:, RB + 1] = jnp.where(b < BANDS - 1, x1s[:, RB + 1], nothing)
+    for f in range(FR):
+        widen(f, 0, jnp.where(b > 0, x1s[f, 0].astype(F32), 0.0))
+        widen(f, RB + 1, jnp.where(b < BANDS - 1, x1s[f, RB + 1].astype(F32), 0.0))
+
+    def upsample(f, c):
+        for r2 in range(2):
+            y = []
+            for c2 in range(2):
+                acc = None
+                for rt in range(2):
+                    x = x3[f, r2 + rt : r2 + rt + RB, :, c2 * C_MID : (c2 + 2) * C_MID].reshape(RB * COLS, 2 * C_MID)
+                    d = lax.dot_general(
+                        x, u[r2 * 2 + c2, :, rt * 2 * C_MID : (rt + 1) * 2 * C_MID],
+                        (((1,), (1,)), ((), ())), preferred_element_type=F32,
+                    )
+                    acc = d if acc is None else acc + d
+                y.append(acc)
+            full = jnp.concatenate([y[0][:, :128], y[0][:, 128:] + y[1][:, :128], y[1][:, 128:]], axis=1)
+            for p in range(RB):
+                for l in range(3):
+                    zs[l, pl.ds(2 * p + r2, COLS, stride=8), :] = full[p * COLS : (p + 1) * COLS, l * 128 : (l + 1) * 128]
+        for q in range(COLS):
+            for l in range(3):
+                at = q * 2 * C_OUT + l * 128
+                out[f, :, at : at + 128] = zs[l, q * 8 : (q + 1) * 8, :].astype(BF)
+        return c
+
+    lax.fori_loop(0, FR, upsample, 0)
 
     pl.when(b > 0)(lambda: halo_copy(True).wait_send())
     pl.when(b < BANDS - 1)(lambda: halo_copy(False).wait_send())
@@ -299,49 +353,20 @@
         pl.when(b != tb)(lambda tb=tb: stat_copy(tb).wait_send())
 
 
-def upsample_kernel(x1, u, out, x3, zs):
-    def widen(r, c):
-        v = x1[0, r].astype(F32)
-        for dx, w in enumerate(col_shifts(v)):
-            x3[r, :, dx * C_MID : (dx + 1) * C_MID] = w.astype(BF)
-        return c
-
-    lax.fori_loop(0, RB + 2, widen, 0)
-    for r2 in range(2):
-        y = []
-        for c2 in range(2):
-            acc = None
-            for rt in range(2):
-                x = x3[r2 + rt : r2 + rt + RB, :, c2 * C_MID : (c2 + 2) * C_MID].reshape(RB * COLS, 2 * C_MID)
-                d = lax.dot_general(
-                    x, u[r2 * 2 + c2, :, rt * 2 * C_MID : (rt + 1) * 2 * C_MID],
-                    (((1,), (1,)), ((), ())), preferred_element_type=F32,
-                )
-                acc = d if acc is None else acc + d
-            y.append(acc)
-        full = jnp.concatenate([y[0][:, :128], y[0][:, 128:] + y[1][:, :128], y[1][:, 128:]], axis=1)
-        for p in range(RB):
-            for l in range(3):
-                zs[l, pl.ds(2 * p + r2, COLS, stride=8), :] = full[p * COLS : (p + 1) * COLS, l * 128 : (l + 1) * 128]
-
-    for q in range(COLS):
-        for l in range(3):
-            at = q * 2 * C_OUT + l * 128
-            out[0, :, at : at + 128] = zs[l, q * 8 : (q + 1) * 8, :].astype(BF)
-
-
 def local(segs, latents, weight_in, weight_mid, weight_up, norm_gain, norm_shift):
-    z = latents.reshape(8, COLS, C_LAT).transpose(1, 0, 2).reshape(COLS, 8 * C_LAT)
-    vm = pl.BlockSpec(memory_space=pltpu.VMEM)
-    x1, u = pl.pallas_call(
-        functools.partial(features_kernel, segs),
-        out_shape=(
-            jax.ShapeDtypeStruct((FR, RB + 2, COLS, C_MID), BF),
-            jax.ShapeDtypeStruct((4, 256, 4 * C_MID), BF),
-        ),
-        in_specs=[vm, vm, pl.BlockSpec(memory_space=pl.ANY), vm, vm, vm],
-        out_specs=(vm, vm),
+    operands = (latents, weight_in, weight_mid, weight_up.T, norm_gain, norm_shift)
+    return pl.pallas_call(
+        functools.partial(decoder_kernel, segs),
+        out_shape=pltpu.VMEM((FR, 2 * RB, 2 * COLS * C_OUT), BF),
+        in_specs=[pl.BlockSpec(memory_space=pltpu.HBM)] * 6,
+        out_specs=pl.BlockSpec(memory_space=pltpu.VMEM),
         scratch_shapes=[
+            pltpu.VMEM((8, COLS * C_LAT), BF),
+            pltpu.VMEM((C_MID,), F32),
+            pltpu.VMEM((C_MID,), F32),
+            pltpu.VMEM((3, 9 * C_LAT, C_MID), BF),
+            pltpu.VMEM((C_OUT, 9 * C_MID), BF),
+            pltpu.VMEM((COLS, 128), BF),
             pltpu.VMEM((12, COLS, 128), BF),
             pltpu.VMEM((4 * COLS, 3 * 384), BF),
             pltpu.VMEM((3, 3 * 384, 2 * C_MID), BF),
@@ -352,7 +377,10 @@
             pltpu.VMEM((BANDS, 8, C_MID), F32),
             pltpu.VMEM((4, RB + 2, COLS, TAPW), BF),
             pltpu.VMEM((FR, RB + 2, COLS, C_MID), BF),
-            pltpu.SemaphoreType.DMA,
+            pltpu.VMEM((4, 256, 4 * C_MID), BF),
+            pltpu.VMEM((FR, RB + 2, COLS, TAPW), BF),
+            pltpu.VMEM((3, COLS * 8, 128), F32),
+            pltpu.SemaphoreType.DMA((6,)),
             pltpu.SemaphoreType.DMA((12,)),
             pltpu.SemaphoreType.DMA((12,)),
             pltpu.SemaphoreType.DMA((BANDS,)),
@@ -360,25 +388,9 @@
             pltpu.SemaphoreType.DMA((2,)),
             pltpu.SemaphoreType.DMA((2,)),
         ],
-        compiler_params=pltpu.CompilerParams(collective_id=0, has_side_effects=True, vmem_limit_bytes=56 << 20),
-        name="features",
-    )(z, weight_in, weight_mid, weight_up.T, norm_gain, norm_shift)
-    return pl.pallas_call(
-        upsample_kernel,
-        grid=(FR,),
-        out_shape=jax.ShapeDtypeStruct((FR, 2 * RB, 2 * COLS * C_OUT), BF),
-        in_specs=[
-            pl.BlockSpec((1, RB + 2, COLS, C_MID), lambda f: (f, 0, 0, 0)),
-            pl.BlockSpec((4, 256, 4 * C_MID), lambda f: (0, 0, 0)),
-        ],
-        out_specs=pl.BlockSpec((1, 2 * RB, 2 * COLS * C_OUT), lambda f: (f, 0, 0)),
-        scratch_shapes=[
-            pltpu.VMEM((RB + 2, COLS, TAPW), BF),
-            pltpu.VMEM((3, COLS * 8, 128), F32),
-        ],
-        compiler_params=pltpu.CompilerParams(vmem_limit_bytes=40 << 20),
-        name="upsample",
-    )(x1, u)
+        compiler_params=pltpu.CompilerParams(collective_id=0, has_side_effects=True, vmem_limit_bytes=58 << 20),
+        name="decoder",
+    )(*(pltpu.with_memory_space_constraint(x, pltpu.HBM) for x in operands))
 
 
 def solution(mesh):

time: 50.7 us -> 40.9 us (0.81)
  Pallas kernels: 45.1 us -> 39.4 us
  local copies, waits for them, and re-layouts: 5.22 us -> 1.27 us
    pallas_call x2 -> x1, Pallas kernels: 45.1 us -> 39.4 us  [local(): pl.pallas_call(functools.partial(decoder_kernel, segs), out_shape=pltpu.V...]
    unnamed x4 -> x1, local copies, waits for them, and re-layouts: 3.26 us -> 1.27 us
    reshape x2 -> x0, local copies, waits for them, and re-layouts: 1.78 us -> none  [local(): latents.reshape(8, COLS, C_LAT).transpose(1, 0, 2).reshape(COLS, 8 * C_LAT)]
where the time goes in v1:
time: 40.9 us; the launch traced here: 40.7 us
  Pallas kernels  39.4 us (96%)
  local copies, waits for them, and re-layouts  1.27 us (3%)
    pallas_call x1, Pallas kernels, local(): pl.pallas_call(functools.partial(decoder_kernel, segs), out_shape=pltpu.V...  39.4 us
    unnamed x1, local copies, waits for them, and re-layouts  1.27 us

profile of v1, /device:TPU:65, one launch (start us, length us, event | category | flops | bytes accessed | tf_op | source)
XLA Modules:
  0.0 40.7 jit_solution(1041350586897457199)
XLA Ops:
  0.0 39.4 %decoder.1 = bf16[2,8,61440]{2,1,0:T(8,128)(2,1)S(1)} custom-call(bf16[8,2560]{1,0:T(8,128)(2,1)} %lat_hbm.1, bf16[3,144,384]{2,1,0:T(8,128)(2,1)} %w_in_hbm.1, bf16[3,3456,384]{2,1,0:T(8,128)(2,1)} %w_mid.1, bf16[192,3456]{1,0:T(8,128)(2,1)} %bitcast.1, f32[384]{0:T(512)} %gain_hbm.1, f32[384]{0:T(512)} %shift_hbm.1), custom_call_target="tpu_custom_call" | custom-call | tf_op jit(solution)/shard_map/decoder/pallas_call | solution.py:358
  39.4 1.3 %copy.8 = bf16[2,8,61440]{2,1,0:T(8,128)(2,1)} copy(bf16[2,8,61440]{2,1,0:T(8,128)(2,1)S(1)} %decoder.1) | data formatting | bytes 3932160

commit v2 on v1

--- a/solution.py
+++ b/solution.py
@@ -19,6 +19,8 @@
 CELLS = HL * COLS * (C_MID // GROUPS)
 TAPW = 3 * C_MID
 PAIRS = ((1, 2), (3, 4), (0, 5))
+EARLY = 40
+MADE = [(i, k) for i in range(4) for k in range(4) if i in (1, 2) or k in (1, 2)]
 MESH = pl.DeviceIdType.MESH
 BF = jnp.bfloat16
 F32 = jnp.float32
@@ -47,7 +49,7 @@
 
 def decoder_kernel(
     segs, lat_hbm, w_in_hbm, w_mid, w_up_hbm, gain_hbm, shift_hbm, out,
-    lat, gain, shift, w_in, w_upt, z, lrecv, lst, wb, x0s, wm, gs, st_src, st_recv, v3, x1s, u, x3, zs,
+    lat, gain, shift, w_in, w_upt, z, lrecv, lst, wb, x0s, act, wm, hs, st_src, st_recv, taps, prod, ysum, rsum, x1s, u, zs,
     wsem, lsend_sem, lrecv_sem, ssend_sem, srecv_sem, hsend_sem, hrecv_sem,
 ):
     s = lax.axis_index("seg")
@@ -128,33 +130,37 @@
 
     load_up.wait()
     sets = (((0,), (1, 2)), ((0, 1), (2,)))
-    for r2 in range(2):
-        for c2 in range(2):
-            ph = r2 * 2 + c2
-            for rt in range(2):
-                for ct in range(2):
-                    acc = None
-                    for dy in sets[r2][rt]:
-                        for dx in sets[c2][ct]:
-                            w = w_upt[:, (dy * 3 + dx) * C_MID : (dy * 3 + dx + 1) * C_MID].astype(F32)
-                            acc = w if acc is None else acc + w
-                    k0 = (rt * 2 + ct) * C_MID
-                    n0 = 64 * c2
-                    u[ph, n0 : n0 + C_OUT, k0 : k0 + C_MID] = acc.astype(BF)
+    for c2 in range(2):
+        for m, (rows, sign) in enumerate((((0, 1, 2), 1.0), ((0,), -1.0), ((2,), 1.0))):
+            n0 = 64 * c2
+            for ct in range(2):
+                acc = None
+                for dy in rows:
+                    for dx in sets[c2][ct]:
+                        w = w_upt[:, (dy * 3 + dx) * C_MID : (dy * 3 + dx + 1) * C_MID].astype(F32)
+                        acc = w if acc is None else acc + w
+                u[c2 * 3 + m, n0 : n0 + C_OUT, ct * C_MID : (ct + 1) * C_MID] = (acc * sign).astype(BF)
             z0 = C_OUT if c2 == 0 else 0
-            u[ph, z0 : z0 + 64, :] = jnp.zeros((64, 4 * C_MID), BF)
+            u[c2 * 3 + m, z0 : z0 + 64, :] = jnp.zeros((64, 2 * C_MID), BF)
 
     load_w.wait()
 
-    def combine(i, c):
-        rows = pl.ds(pl.multiple_of(i * 128, 128), 128)
-        w0, w1, w2 = (wm[t, rows, :].astype(F32) for t in range(3))
-        outer, mid = (w0 + w2) * 0.5, w1 * 0.5
-        gs[0, rows, :] = (outer + mid).astype(BF)
-        gs[1, rows, :] = (outer - mid).astype(BF)
-        return c
-
-    lax.fori_loop(0, 27, combine, 0)
+    def combos(g):
+        outer, mid = (g[0] + g[2]) * 0.5, g[1] * 0.5
+        return g[0], outer + mid, outer - mid, g[2]
+
+    def combine(c, carry):
+        at = pl.multiple_of(c * 16, 16)
+        by_dy = []
+        for dy in range(3):
+            by_dy.append(combos([wm[t, pl.ds(dy * TAPW + at, 16), :].astype(F32) for t in range(3)]))
+        for i in range(4):
+            for k, h in enumerate(combos([by_dy[dy][i] for dy in range(3)])):
+                if (i, k) in MADE:
+                    hs[MADE.index((i, k)), pl.ds(at, 16), :] = h.astype(BF)
+        return carry
+
+    lax.fori_loop(0, EARLY, combine, 0)
 
     def arrived(slot):
         pltpu.make_async_remote_copy(
@@ -183,11 +189,11 @@
         both = jnp.concatenate([lrecv[2 * g].astype(F32), lrecv[2 * g + 1].astype(F32)], axis=1)
         win = pltpu.roll(both, lax.rem(32 - 64 * b + 256, 256), 1)[:, :128]
         win = jnp.where(jnp.logical_and(in_frame, 2 * s - 4 + g >= 0), win, 0.0)
-        taps = jnp.concatenate(col_shifts(win), axis=1).astype(BF)
+        near = jnp.concatenate(col_shifts(win), axis=1).astype(BF)
         for f in range(4):
             t = g - f
             if 0 <= t < 3:
-                lst[f * COLS : (f + 1) * COLS, t * 384 : (t + 1) * 384] = taps
+                lst[f * COLS : (f + 1) * COLS, t * 384 : (t + 1) * 384] = near
 
     def conv_in(q):
         return jnp.dot(lst[...], wb[q], preferred_element_type=F32).astype(BF)
@@ -223,6 +229,8 @@
     for f in range(4):
         for k, r in enumerate(PAIRS[2]):
             x0s[f, r] = x0[f * COLS : (f + 1) * COLS, k * C_MID : (k + 1) * C_MID]
+
+    lax.fori_loop(EARLY, TAPW // 16, combine, 0)
 
     def stats_in(ob):
         pltpu.make_async_remote_copy(
@@ -251,103 +259,180 @@
     add = (shift[...].reshape(1, C_MID) - mean * mul) * 0.5
     mul = mul * 0.5
 
-    def activate(r, c):
+    def activate(f, r):
         arow = 4 * b - 1 + r
-        row_ok = jnp.logical_and(arow >= 0, arow < HL)
-        a = []
-        for f in range(4):
-            ok = jnp.where(jnp.logical_and(row_ok, 2 * s - 2 + f >= 0), 1.0, 0.0)
-            hv = x0s[f, r].astype(F32) * (mul[f : f + 1] * ok) + add[f : f + 1] * ok
-            a.append(hv + hv * jnp.tanh(hv))
-        for i, v in enumerate((a[0] - a[2], a[1] + a[2], a[2] - a[1], a[1] - a[3])):
-            for dx, w in enumerate(col_shifts(v)):
-                v3[i, r, :, dx * C_MID : (dx + 1) * C_MID] = w.astype(BF)
+        ok = jnp.logical_and(jnp.logical_and(arow >= 0, arow < HL), 2 * s - 2 + f >= 0)
+        ok = jnp.where(ok, 1.0, 0.0)
+        hv = x0s[f, r].astype(F32) * (mul[f : f + 1] * ok) + add[f : f + 1] * ok
+        act[f, r] = (hv + hv * jnp.tanh(hv)).astype(BF)
+
+    def spread(slot, v):
+        for dx, w in enumerate(col_shifts(v)):
+            taps[slot, :, dx * C_MID : (dx + 1) * C_MID] = w.astype(BF)
+
+    def inputs(i, tau):
+        v = []
+        for r in range(4):
+            m, n, sign = ((0, 2, -1), (1, 2, 1), (2, 1, -1), (1, 3, -1))[i]
+            am, an = act[m, 2 * tau + r].astype(F32), act[n, 2 * tau + r].astype(F32)
+            v.append(am + an if sign > 0 else am - an)
+        for k, w in enumerate((v[0] - v[2], v[1] + v[2], v[2] - v[1], v[1] - v[3])):
+            spread(i * 8 + k * 2 + tau, w)
+
+    def product(i, k):
+        if (i, k) in MADE:
+            g = hs[MADE.index((i, k))]
+        else:
+            at = 0 if k == 0 else 2 * TAPW
+            g = wm[0 if i == 0 else 2, at : at + TAPW, :]
+        at = i * 8 + k * 2
+        to = prod.at[i % 2, k % 2]
+        to[...] = jnp.dot(taps[at : at + 2].reshape(2 * COLS, TAPW), g, preferred_element_type=F32)
+        return to
+
+    def add_to(sums, k, to):
+        if k == 0:
+            sums[0] = to[...]
+        elif k == 1:
+            sums[0] += to[...]
+            sums[1] = to[...]
+        elif k == 2:
+            sums[0] += to[...]
+            sums[1] -= to[...]
+        else:
+            sums[1] -= to[...]
+
+    def middle(r, c):
+        activate(1, r)
+        activate(2, r)
         return c
 
-    lax.fori_loop(0, 6, activate, 0)
-
-    def halo_copy(up):
+    lax.fori_loop(0, RB + 2, middle, 0)
+
+    def first_inputs(tau, c):
+        inputs(1, tau)
+        return c
+
+    lax.fori_loop(0, 2, first_inputs, 0)
+
+    def stage(i, sums, beside):
+        for k in range(4):
+            add_to(sums, k, product(i, k))
+            for fn in beside[k]:
+                fn()
+
+    def later(fn, *args):
+        return functools.partial(fn, *args)
+
+    def outer_work(i):
+        rows = [later(activate, i, r) for r in range(RB + 2)]
+        return rows[:3], rows[3:], [later(inputs, i, 0)], [later(inputs, i, 1)]
+
+    stage(1, ysum.at[0], ([later(inputs, 2, 0)], [later(inputs, 2, 1)], [], []))
+    stage(2, ysum.at[1], outer_work(0))
+    for par in range(2):
+        t1, t2 = ysum[0, par], ysum[1, par]
+        ysum[0, par] = t1 + t2
+        ysum[1, par] = t1 - t2
+
+    def x3_slot(f, p):
+        return f * 7 + p
+
+    def d3_slot(f, p):
+        return {0: 14, RB: 16}[p] + f if p in (0, RB) else f * 7 + RB + p - 1
+
+    def halo_copy(f, up):
         return pltpu.make_async_remote_copy(
-            src_ref=x1s.at[:, 1 if up else RB],
-            dst_ref=x1s.at[:, RB + 1 if up else 0],
-            send_sem=hsend_sem.at[0 if up else 1],
-            recv_sem=hrecv_sem.at[0 if up else 1],
+            src_ref=x1s.at[f, 1 if up else RB],
+            dst_ref=x1s.at[f, RB + 1 if up else 0],
+            send_sem=hsend_sem.at[f, 0 if up else 1],
+            recv_sem=hrecv_sem.at[f, 0 if up else 1],
             device_id={"seg": s, "band": b - 1 if up else b + 1},
             device_id_type=MESH,
         )
 
-    def widen(f, r, v):
-        for dx, w in enumerate(col_shifts(v)):
-            x3[f, r, :, dx * C_MID : (dx + 1) * C_MID] = w.astype(BF)
-
-    def residual(h, c):
-        ra, rb = h, 3 - h
-
-        def product(i):
-            acc = None
-            for dy in range(3):
-                x = jnp.concatenate([v3[i, ra + dy], v3[i, rb + dy]], axis=0)
-                ks = slice(dy * TAPW, (dy + 1) * TAPW)
-                g = (wm[0, ks, :], gs[0, ks, :], gs[1, ks, :], wm[2, ks, :])[i]
-                d = jnp.dot(x, g, preferred_element_type=F32)
-                acc = d if acc is None else acc + d
-            return acc
-
-        t1, t2, t3, t4 = (product(i) for i in range(4))
-        for f, y in enumerate((t1 + t2 + t3, t2 - t3 - t4)):
-            for r, part in ((ra, y[:COLS]), (rb, y[COLS:])):
-                x1 = (x0s[FR + f, 1 + r].astype(F32) + part).astype(BF)
-                x1s[f, 1 + r] = x1
-                widen(f, 1 + r, x1.astype(F32))
-
-        @pl.when(h == 0)
-        def _():
-            pl.when(b > 0)(lambda: halo_copy(True).start())
-            pl.when(b < BANDS - 1)(lambda: halo_copy(False).start())
-
-        return c
-
-    lax.fori_loop(0, 2, residual, 0)
-
-    @pl.when(b > 0)
-    def _():
-        halo_copy(False).wait_recv()
-
-    @pl.when(b < BANDS - 1)
-    def _():
-        halo_copy(True).wait_recv()
-
-    for f in range(FR):
-        widen(f, 0, jnp.where(b > 0, x1s[f, 0].astype(F32), 0.0))
-        widen(f, RB + 1, jnp.where(b < BANDS - 1, x1s[f, RB + 1].astype(F32), 0.0))
-
-    def upsample(f, c):
-        for r2 in range(2):
-            y = []
-            for c2 in range(2):
-                acc = None
-                for rt in range(2):
-                    x = x3[f, r2 + rt : r2 + rt + RB, :, c2 * C_MID : (c2 + 2) * C_MID].reshape(RB * COLS, 2 * C_MID)
-                    d = lax.dot_general(
-                        x, u[r2 * 2 + c2, :, rt * 2 * C_MID : (rt + 1) * 2 * C_MID],
-                        (((1,), (1,)), ((), ())), preferred_element_type=F32,
-                    )
-                    acc = d if acc is None else acc + d
-                y.append(acc)
-            full = jnp.concatenate([y[0][:, :128], y[0][:, 128:] + y[1][:, :128], y[1][:, 128:]], axis=1)
-            for p in range(RB):
-                for l in range(3):
-                    zs[l, pl.ds(2 * p + r2, COLS, stride=8), :] = full[p * COLS : (p + 1) * COLS, l * 128 : (l + 1) * 128]
+    def finish(f, beside):
+        stage(3 * f, rsum, beside)
+        for par in range(2):
+            y = ysum[f, par] + rsum[par] if f == 0 else ysum[f, par] - rsum[par]
+            for tau in range(2):
+                r = 1 + 2 * tau + par
+                x1s[f, r] = (x0s[FR + f, r].astype(F32) + y[tau * COLS : (tau + 1) * COLS]).astype(BF)
+
+    def send(f):
+        pl.when(b > 0)(lambda: halo_copy(f, True).start())
+        pl.when(b < BANDS - 1)(lambda: halo_copy(f, False).start())
+
+    def receive(f):
+        pl.when(b > 0)(lambda: halo_copy(f, False).wait_recv())
+        pl.when(b < BANDS - 1)(lambda: halo_copy(f, True).wait_recv())
+
+    def own_taps(f):
+        rows = [x1s[f, 1 + p].astype(F32) for p in range(RB)]
+        for p in range(RB):
+            spread(x3_slot(f, p), rows[p])
+            if p:
+                spread(d3_slot(f, p), rows[p] - rows[p - 1])
+
+    def edge_taps(f):
+        above = jnp.where(b > 0, x1s[f, 0].astype(F32), 0.0)
+        below = jnp.where(b < BANDS - 1, x1s[f, RB + 1].astype(F32), 0.0)
+        spread(d3_slot(f, 0), x1s[f, 1].astype(F32) - above)
+        spread(d3_slot(f, RB), below - x1s[f, RB].astype(F32))
+
+    def phase(c2, m, slot, rows):
+        x = taps[slot : slot + rows, :, c2 * C_MID : (c2 + 2) * C_MID].reshape(rows * COLS, 2 * C_MID)
+        return lax.dot_general(x, u[c2 * 3 + m], (((1,), (1,)), ((), ())), preferred_element_type=F32)
+
+    def place(f, r2, p0, y):
+        full = (y[0][:, :128], y[0][:, 128:] + y[1][:, :128], y[1][:, 128:])
+        for p in range(y[0].shape[0] // COLS):
+            for l in range(3):
+                at = pl.ds(2 * (p0 + p) + r2, COLS, stride=8)
+                zs[f, l, at, :] = full[l][p * COLS : (p + 1) * COLS]
+
+    def inner_rows(f):
+        even, odd = [], []
+        for c2 in range(2):
+            mid = phase(c2, 0, x3_slot(f, 0), RB)
+            even.append(mid[COLS:] + phase(c2, 1, d3_slot(f, 1), RB - 1))
+            odd.append(mid[:-COLS] + phase(c2, 2, d3_slot(f, 1), RB - 1))
+            prod[f, c2, :COLS, :256] = mid[:COLS]
+            prod[f, c2, COLS:, :256] = mid[-COLS:]
+        place(f, 0, 1, even)
+        place(f, 1, 0, odd)
+
+    def edge_rows():
+        for e, (m, p, row) in enumerate(((1, 0, 0), (2, RB, RB - 1))):
+            d = [phase(c2, m, d3_slot(0, p), FR) for c2 in range(2)]
+            for f in range(FR):
+                y = [prod[f, c2, e * COLS : (e + 1) * COLS, :256] + d[c2][f * COLS : (f + 1) * COLS] for c2 in range(2)]
+                place(f, e, row, y)
+
+    def pack(f):
         for q in range(COLS):
             for l in range(3):
                 at = q * 2 * C_OUT + l * 128
-                out[f, :, at : at + 128] = zs[l, q * 8 : (q + 1) * 8, :].astype(BF)
-        return c
-
-    lax.fori_loop(0, FR, upsample, 0)
-
-    pl.when(b > 0)(lambda: halo_copy(True).wait_send())
-    pl.when(b < BANDS - 1)(lambda: halo_copy(False).wait_send())
+                out[f, :, at : at + 128] = zs[f, l, q * 8 : (q + 1) * 8, :].astype(BF)
+
+    finish(0, outer_work(3))
+    send(0)
+    finish(1, ([], [], [later(own_taps, 0)], []))
+    send(1)
+    own_taps(1)
+    inner_rows(0)
+    inner_rows(1)
+    for f in range(FR):
+        receive(f)
+    for f in range(FR):
+        edge_taps(f)
+    edge_rows()
+    for f in range(FR):
+        pack(f)
+
+    for f in range(FR):
+        pl.when(b > 0)(lambda f=f: halo_copy(f, True).wait_send())
+        pl.when(b < BANDS - 1)(lambda f=f: halo_copy(f, False).wait_send())
     each_latent_copy(lambda ds, tb: latent_copy(ds, tb).wait_send())
     for tb in range(BANDS):
         pl.when(b != tb)(lambda tb=tb: stat_copy(tb).wait_send())
@@ -371,24 +456,27 @@
             pltpu.VMEM((4 * COLS, 3 * 384), BF),
             pltpu.VMEM((3, 3 * 384, 2 * C_MID), BF),
             pltpu.VMEM((4, RB + 2, COLS, C_MID), BF),
+            pltpu.VMEM((4, RB + 2, COLS, C_MID), BF),
             pltpu.VMEM((3, 9 * C_MID, C_MID), BF),
-            pltpu.VMEM((2, 9 * C_MID, C_MID), BF),
+            pltpu.VMEM((len(MADE), TAPW, C_MID), BF),
             pltpu.VMEM((8, C_MID), F32),
             pltpu.VMEM((BANDS, 8, C_MID), F32),
-            pltpu.VMEM((4, RB + 2, COLS, TAPW), BF),
+            pltpu.VMEM((32, COLS, TAPW), BF),
+            pltpu.VMEM((2, 2, 2 * COLS, C_MID), F32),
+            pltpu.VMEM((FR, 2, 2 * COLS, C_MID), F32),
+            pltpu.VMEM((2, 2 * COLS, C_MID), F32),
             pltpu.VMEM((FR, RB + 2, COLS, C_MID), BF),
-            pltpu.VMEM((4, 256, 4 * C_MID), BF),
-            pltpu.VMEM((FR, RB + 2, COLS, TAPW), BF),
-            pltpu.VMEM((3, COLS * 8, 128), F32),
+            pltpu.VMEM((6, 256, 2 * C_MID), BF),
+            pltpu.VMEM((FR, 3, COLS * 8, 128), F32),
             pltpu.SemaphoreType.DMA((6,)),
             pltpu.SemaphoreType.DMA((12,)),
             pltpu.SemaphoreType.DMA((12,)),
             pltpu.SemaphoreType.DMA((BANDS,)),
             pltpu.SemaphoreType.DMA((BANDS,)),
-            pltpu.SemaphoreType.DMA((2,)),
-            pltpu.SemaphoreType.DMA((2,)),
+            pltpu.SemaphoreType.DMA((FR, 2)),
+            pltpu.SemaphoreType.DMA((FR, 2)),
         ],
-        compiler_params=pltpu.CompilerParams(collective_id=0, has_side_effects=True, vmem_limit_bytes=58 << 20),
+        compiler_params=pltpu.CompilerParams(collective_id=0, has_side_effects=True, vmem_limit_bytes=60 << 20),
         name="decoder",
     )(*(pltpu.with_memory_space_constraint(x, pltpu.HBM) for x in operands))
 

time: 40.9 us -> 39.1 us (0.956)
  Pallas kernels: 39.4 us -> 37.7 us
    pallas_call x1, Pallas kernels: 39.4 us -> 37.7 us  [local(): pl.pallas_call(functools.partial(decoder_kernel, segs), out_shape=pltpu.V...]
where the time goes in v2:
time: 39.1 us; the launch traced here: 39 us
  Pallas kernels  37.7 us (96%)
  local copies, waits for them, and re-layouts  1.27 us (3%)
    pallas_call x1, Pallas kernels, local(): pl.pallas_call(functools.partial(decoder_kernel, segs), out_shape=pltpu.V...  37.7 us
    unnamed x1, local copies, waits for them, and re-layouts  1.27 us

profile of v2, /device:TPU:65, one launch (start us, length us, event | category | flops | bytes accessed | tf_op | source)
XLA Modules:
  0.0 39.0 jit_solution(6969309104203153740)
XLA Ops:
  0.0 37.7 %decoder.1 = bf16[2,8,61440]{2,1,0:T(8,128)(2,1)S(1)} custom-call(bf16[8,2560]{1,0:T(8,128)(2,1)} %lat_hbm.1, bf16[3,144,384]{2,1,0:T(8,128)(2,1)} %w_in_hbm.1, bf16[3,3456,384]{2,1,0:T(8,128)(2,1)} %w_mid.1, bf16[192,3456]{1,0:T(8,128)(2,1)} %bitcast.1, f32[384]{0:T(512)} %gain_hbm.1, f32[384]{0:T(512)} %shift_hbm.1), custom_call_target="tpu_custom_call" | custom-call | tf_op jit(solution)/shard_map/decoder/pallas_call | solution.py:443
  37.7 1.3 %copy.8 = bf16[2,8,61440]{2,1,0:T(8,128)(2,1)} copy(bf16[2,8,61440]{2,1,0:T(8,128)(2,1)S(1)} %decoder.1) | data formatting | bytes 3932160

commit v3 on v2

--- a/solution.py
+++ b/solution.py
@@ -19,6 +19,7 @@
 CELLS = HL * COLS * (C_MID // GROUPS)
 TAPW = 3 * C_MID
 PAIRS = ((1, 2), (3, 4), (0, 5))
+QC = COLS // 4
 EARLY = 40
 MADE = [(i, k) for i in range(4) for k in range(4) if i in (1, 2) or k in (1, 2)]
 MESH = pl.DeviceIdType.MESH
@@ -44,7 +45,21 @@
         from_below = pltpu.roll(pltpu.roll(x, k * C_LAT, 2), 8 - k, 1)
         from_above = pltpu.roll(pltpu.roll(x, 128 - k * C_LAT, 2), k, 1)
         x = jnp.where(r == c, x, jnp.where(r < c, from_below, from_above))
-    return x.reshape(COLS, 128).astype(BF)
+    x = x.reshape(COLS, 128)
+    return [x[q * QC : (q + 1) * QC] for q in range(4)]
+
+
+def swap_quarters(x):
+    group = lax.broadcasted_iota(jnp.int32, (QC, 128), 1) // 32
+    x = list(x)
+    for m in (1, 2):
+        bit = (group // m) % 2
+        for q in range(4):
+            if not q & m:
+                lo, hi = x[q], x[q | m]
+                x[q] = jnp.where(bit == 0, lo, pltpu.roll(hi, m * 32, 1))
+                x[q | m] = jnp.where(bit == 1, hi, pltpu.roll(lo, 128 - m * 32, 1))
+    return x
 
 
 def decoder_kernel(
@@ -85,7 +100,8 @@
 
     each_peer(greet)
     load_lat.wait()
-    z[...] = columns_first(lat)
+    for k, v in enumerate(swap_quarters(columns_first(lat))):
+        z[k] = v.astype(BF)
 
     load_in.wait()
     for q, pair in enumerate(PAIRS):
@@ -103,10 +119,13 @@
 
     pl.semaphore_wait(barrier, peers)
 
-    def latent_copy(ds, tb):
+    needs = {(0, 0): (0, 1, 3), (0, 1): (1, 0, 3), (0, 2): (3, 0, 1), (1, 1): (0, 3, 1), (1, 2): (0, 1, 3), (1, 3): (1, 0, 3)}
+
+    def latent_copy(ds, tb, h):
+        src, dst, n = needs[h, tb]
         return pltpu.make_async_remote_copy(
-            src_ref=z,
-            dst_ref=lrecv.at[8 - 4 * ds + b],
+            src_ref=z.at[src : src + n],
+            dst_ref=lrecv.at[4 - 2 * ds + b // 2, dst : dst + n],
             send_sem=lsend_sem.at[ds * BANDS + tb],
             recv_sem=lrecv_sem.at[8 - 4 * ds + b],
             device_id={"seg": s + ds, "band": jnp.int32(tb)},
@@ -115,18 +134,20 @@
 
     def each_latent_copy(fn):
         for ds in range(3):
-            for tb in range(BANDS):
-                ok = s + ds < segs
-                if tb == 0:
-                    ok = jnp.logical_and(ok, half == 0)
-                if tb == BANDS - 1:
-                    ok = jnp.logical_and(ok, half == 1)
+            for h, tb in needs:
+                ok = jnp.logical_and(s + ds < segs, half == h)
                 if ds == 0:
                     ok = jnp.logical_and(ok, b != tb)
-                pl.when(ok)(functools.partial(fn, ds, tb))
-
-    each_latent_copy(lambda ds, tb: latent_copy(ds, tb).start())
-    lrecv[8 + b] = z[...]
+                pl.when(ok)(functools.partial(fn, ds, tb, h))
+
+    each_latent_copy(lambda ds, tb, h: latent_copy(ds, tb, h).start())
+
+    def keep(tb):
+        src, dst, n = needs[tb % 2, tb]
+        lrecv[4 + tb // 2, dst : dst + n] = z[src : src + n]
+
+    for tb in range(BANDS):
+        pl.when(b == tb)(functools.partial(keep, tb))
 
     load_up.wait()
     sets = (((0,), (1, 2)), ((0, 1), (2,)))
@@ -162,32 +183,28 @@
 
     lax.fori_loop(0, EARLY, combine, 0)
 
-    def arrived(slot):
+    def arrived(g, h, tb):
+        src, dst, n = needs[h, tb]
         pltpu.make_async_remote_copy(
-            src_ref=z,
-            dst_ref=lrecv.at[slot],
+            src_ref=z.at[src : src + n],
+            dst_ref=lrecv.at[g, dst : dst + n],
             send_sem=lsend_sem.at[0],
-            recv_sem=lrecv_sem.at[slot],
+            recv_sem=lrecv_sem.at[2 * g + h],
             device_id={"seg": s, "band": b},
             device_id_type=MESH,
         ).wait_recv()
 
-    for slot in range(12):
-        ok = s - 2 + slot // 4 >= 0
-        if slot % 2 == 0:
-            ok = jnp.logical_and(ok, b <= 2)
-        else:
-            ok = jnp.logical_and(ok, b >= 1)
-        if slot >= 8:
-            ok = jnp.logical_and(ok, b != slot - 8)
-        pl.when(ok)(functools.partial(arrived, slot))
+    for g in range(6):
+        for h, tb in needs:
+            ok = jnp.logical_and(s - 2 + g // 2 >= 0, b == tb)
+            if (g - 4) * 2 + h != tb:
+                pl.when(ok)(functools.partial(arrived, g, h, tb))
 
     lane = lax.broadcasted_iota(jnp.int32, (COLS, 128), 1)
     row = 4 * b - 2 + lane // 16
     in_frame = jnp.logical_and(row >= 0, row < HL)
     for g in range(6):
-        both = jnp.concatenate([lrecv[2 * g].astype(F32), lrecv[2 * g + 1].astype(F32)], axis=1)
-        win = pltpu.roll(both, lax.rem(32 - 64 * b + 256, 256), 1)[:, :128]
+        win = jnp.concatenate(swap_quarters([lrecv[g, k].astype(F32) for k in range(4)]), axis=0)
         win = jnp.where(jnp.logical_and(in_frame, 2 * s - 4 + g >= 0), win, 0.0)
         near = jnp.concatenate(col_shifts(win), axis=1).astype(BF)
         for f in range(4):
@@ -433,7 +450,7 @@
     for f in range(FR):
         pl.when(b > 0)(lambda f=f: halo_copy(f, True).wait_send())
         pl.when(b < BANDS - 1)(lambda f=f: halo_copy(f, False).wait_send())
-    each_latent_copy(lambda ds, tb: latent_copy(ds, tb).wait_send())
+    each_latent_copy(lambda ds, tb, h: latent_copy(ds, tb, h).wait_send())
     for tb in range(BANDS):
         pl.when(b != tb)(lambda tb=tb: stat_copy(tb).wait_send())
 
@@ -451,8 +468,8 @@
             pltpu.VMEM((C_MID,), F32),
             pltpu.VMEM((3, 9 * C_LAT, C_MID), BF),
             pltpu.VMEM((C_OUT, 9 * C_MID), BF),
-            pltpu.VMEM((COLS, 128), BF),
-            pltpu.VMEM((12, COLS, 128), BF),
+            pltpu.VMEM((4, QC, 128), BF),
+            pltpu.VMEM((6, 4, QC, 128), BF),
             pltpu.VMEM((4 * COLS, 3 * 384), BF),
             pltpu.VMEM((3, 3 * 384, 2 * C_MID), BF),
             pltpu.VMEM((4, RB + 2, COLS, C_MID), BF),

time: 39.1 us -> 37.4 us (0.957)
  Pallas kernels: 37.7 us -> 36 us
    pallas_call x1, Pallas kernels: 37.7 us -> 36 us  [local(): pl.pallas_call(functools.partial(decoder_kernel, segs), out_shape=pltpu.V...]
where the time goes in v3:
time: 37.4 us; the launch traced here: 37.3 us
  Pallas kernels  36 us (96%)
  local copies, waits for them, and re-layouts  1.27 us (3%)
    pallas_call x1, Pallas kernels, local(): pl.pallas_call(functools.partial(decoder_kernel, segs), out_shape=pltpu.V...  36 us
    unnamed x1, local copies, waits for them, and re-layouts  1.27 us

profile of v3, /device:TPU:65, one launch (start us, length us, event | category | flops | bytes accessed | tf_op | source)
XLA Modules:
  0.0 37.3 jit_solution(14875027239822883335)
XLA Ops:
  0.0 36.0 %decoder.1 = bf16[2,8,61440]{2,1,0:T(8,128)(2,1)S(1)} custom-call(bf16[8,2560]{1,0:T(8,128)(2,1)} %lat_hbm.1, bf16[3,144,384]{2,1,0:T(8,128)(2,1)} %w_in_hbm.1, bf16[3,3456,384]{2,1,0:T(8,128)(2,1)} %w_mid.1, bf16[192,3456]{1,0:T(8,128)(2,1)} %bitcast.1, f32[384]{0:T(512)} %gain_hbm.1, f32[384]{0:T(512)} %shift_hbm.1), custom_call_target="tpu_custom_call" | custom-call | tf_op jit(solution)/shard_map/decoder/pallas_call | solution.py:460
  36.0 1.3 %copy.8 = bf16[2,8,61440]{2,1,0:T(8,128)(2,1)} copy(bf16[2,8,61440]{2,1,0:T(8,128)(2,1)S(1)} %decoder.1) | data formatting | bytes 3932160

commit v4 on v3

--- a/solution.py
+++ b/solution.py
@@ -133,7 +133,7 @@
         )
 
     def each_latent_copy(fn):
-        for ds in range(3):
+        for ds in (2, 1, 0):
             for h, tb in needs:
                 ok = jnp.logical_and(s + ds < segs, half == h)
                 if ds == 0:
@@ -287,14 +287,15 @@
         for dx, w in enumerate(col_shifts(v)):
             taps[slot, :, dx * C_MID : (dx + 1) * C_MID] = w.astype(BF)
 
-    def inputs(i, tau):
-        v = []
-        for r in range(4):
-            m, n, sign = ((0, 2, -1), (1, 2, 1), (2, 1, -1), (1, 3, -1))[i]
-            am, an = act[m, 2 * tau + r].astype(F32), act[n, 2 * tau + r].astype(F32)
-            v.append(am + an if sign > 0 else am - an)
-        for k, w in enumerate((v[0] - v[2], v[1] + v[2], v[2] - v[1], v[1] - v[3])):
-            spread(i * 8 + k * 2 + tau, w)
+    def inputs(i, k):
+        m, n, sign = ((0, 2, -1), (1, 2, 1), (2, 1, -1), (1, 3, -1))[i]
+        p, q, plus = ((0, 2, -1), (1, 2, 1), (2, 1, -1), (1, 3, -1))[k]
+        for tau in range(2):
+            v = []
+            for r in (2 * tau + p, 2 * tau + q):
+                am, an = act[m, r].astype(F32), act[n, r].astype(F32)
+                v.append(am + an if sign > 0 else am - an)
+            spread(i * 8 + k * 2 + tau, v[0] + v[1] if plus > 0 else v[0] - v[1])
 
     def product(i, k):
         if (i, k) in MADE:
@@ -326,12 +327,6 @@
 
     lax.fori_loop(0, RB + 2, middle, 0)
 
-    def first_inputs(tau, c):
-        inputs(1, tau)
-        return c
-
-    lax.fori_loop(0, 2, first_inputs, 0)
-
     def stage(i, sums, beside):
         for k in range(4):
             add_to(sums, k, product(i, k))
@@ -341,11 +336,18 @@
     def later(fn, *args):
         return functools.partial(fn, *args)
 
+    def all_inputs(i):
+        return [later(inputs, i, k) for k in range(4)]
+
     def outer_work(i):
         rows = [later(activate, i, r) for r in range(RB + 2)]
-        return rows[:3], rows[3:], [later(inputs, i, 0)], [later(inputs, i, 1)]
-
-    stage(1, ysum.at[0], ([later(inputs, 2, 0)], [later(inputs, 2, 1)], [], []))
+        made = all_inputs(i)
+        return rows[:3], rows[3:], made[:2], made[2:]
+
+    inputs(1, 0)
+    inputs(1, 1)
+    ones, twos = all_inputs(1), all_inputs(2)
+    stage(1, ysum.at[0], (ones[2:3], ones[3:] + twos[:1], twos[1:2], twos[2:]))
     stage(2, ysum.at[1], outer_work(0))
     for par in range(2):
         t1, t2 = ysum[0, par], ysum[1, par]

time: 37.4 us -> 36.5 us (0.976)
  Pallas kernels: 36 us -> 35.1 us
    pallas_call x1, Pallas kernels: 36 us -> 35.1 us  [local(): pl.pallas_call(functools.partial(decoder_kernel, segs), out_shape=pltpu.V...]
where the time goes in v4:
time: 36.5 us; the launch traced here: 36.4 us
  Pallas kernels  35.1 us (96%)
  local copies, waits for them, and re-layouts  1.27 us (3%)
    pallas_call x1, Pallas kernels, local(): pl.pallas_call(functools.partial(decoder_kernel, segs), out_shape=pltpu.V...  35.1 us
    unnamed x1, local copies, waits for them, and re-layouts  1.27 us

profile of v4, /device:TPU:65, one launch (start us, length us, event | category | flops | bytes accessed | tf_op | source)
XLA Modules:
  0.0 36.4 jit_solution(6057974623801268437)
XLA Ops:
  0.0 35.1 %decoder.1 = bf16[2,8,61440]{2,1,0:T(8,128)(2,1)S(1)} custom-call(bf16[8,2560]{1,0:T(8,128)(2,1)} %lat_hbm.1, bf16[3,144,384]{2,1,0:T(8,128)(2,1)} %w_in_hbm.1, bf16[3,3456,384]{2,1,0:T(8,128)(2,1)} %w_mid.1, bf16[192,3456]{1,0:T(8,128)(2,1)} %bitcast.1, f32[384]{0:T(512)} %gain_hbm.1, f32[384]{0:T(512)} %shift_hbm.1), custom_call_target="tpu_custom_call" | custom-call | tf_op jit(solution)/shard_map/decoder/pallas_call | solution.py:462
  35.1 1.3 %copy.8 = bf16[2,8,61440]{2,1,0:T(8,128)(2,1)} copy(bf16[2,8,61440]{2,1,0:T(8,128)(2,1)S(1)} %decoder.1) | data formatting | bytes 3932160
